TPU v7x, 256 devices: a whole 4x4x8 slice. The times are simulated.
256 devices in a mesh: scen: 16 (over y, x), lx: 4 (over z_lo, core), ly: 4 (over z_hi).
Axes of the slice: x: 4, y: 4, z: 8 (z_hi: 4, z_lo: 2; z = z_hi * 2 + z_lo), core: 2. Of those that a mesh axis runs over, the one named last changes fastest.
Arguments:
- density: float32 [16, 512, 2048], P('scen', 'lx', 'ly'), may hold values from 0.2 to 1.5
- trait: float32 [16, 512, 2048], P('scen', 'lx', 'ly'), may hold values from -4 to 4
- variance: float32 [16, 512, 2048], P('scen', 'lx', 'ly'), may hold values from 0.1 to 1
- optimum: float32 [16, 512, 2048], P('scen', 'lx', 'ly'), may hold values from -4 to 4
- observed: float32 [16, 512, 2048], P('scen', 'lx', 'ly'), may hold values from 0 to 1.5
- obs_step: int32 [16, 512], P('scen', 'lx'), may hold values from 1 to 2
- land_code: int32 [512, 2048], P('lx', 'ly'), may hold values 0 or 1
- maps: float32 [2, 512, 2048], P(None, 'lx', 'ly'), may hold values from -4 to 4
- first_moment: float32 [2, 512, 2048], P(None, 'lx', 'ly'), may hold values from -3 to 3
- second_moment: float32 [2, 512, 2048], P(None, 'lx', 'ly'), may hold values from 0.01 to 1
Outputs:
- new_maps: float32 [2, 512, 2048], P(None, 'lx', 'ly')
- new_first: float32 [2, 512, 2048], P(None, 'lx', 'ly')
- new_second: float32 [2, 512, 2048], P(None, 'lx', 'ly')
Inputs may be any that keep to these rules, and one draw needn't show every extreme that they name: `land_code`: 1 marks land, 0 sea.
All inputs are finite; a program needn't handle non-finite values. No bound on the sum of `land_code` on one device may be relied on, other than what follows from the above.
Results may differ from a plain program's by a relative error of at most 0.0003.
Values sent between devices are 32-bit elements; how exact they have to be, the bound alone decides.
A program may use at most 64 MiB of HBM per device.

v0:
```python
import jax
import jax.numpy as jnp
from jax import lax
from jax.sharding import PartitionSpec as P

STEPS = 2
ADAM_STEP = 10
REACH_MAX = 0.2
PRIOR_WEIGHT = 0.1
GROWTH_RATE = 0.5
MUTATION_INPUT = 0.02
LEARN_RATE = 0.01
BETA_FIRST = 0.9
BETA_SECOND = 0.999
ADAM_EPS = 1e-08
LOSS_WEIGHT = 2.0


def extended(block, sides, width):
    for axis, dim in sides:
        count = lax.axis_size(axis)
        forward = [(i, i + 1) for i in range(count - 1)]
        backward = [(target, source) for source, target in forward]
        low = lax.ppermute(
            lax.slice_in_dim(block, block.shape[dim] - width, None, axis=dim), axis, forward
        )
        high = lax.ppermute(lax.slice_in_dim(block, 0, width, axis=dim), axis, backward)
        block = jnp.concatenate([low, block, high], axis=dim)
    return block


def interior(values):
    return values[..., 1:-1, 1:-1]


def advance(fields, raw_maps, optimum_map, land_frac):
    density_now, trait_now, variance_now = (fields[0], fields[1], fields[2])
    reach_map = REACH_MAX * jax.nn.sigmoid(raw_maps[0])
    selection = jax.nn.softplus(interior(raw_maps[1]))
    carried = density_now * trait_now
    moment_two = density_now * (variance_now + trait_now * trait_now)
    reach_mid = interior(reach_map)
    land_mid = interior(land_frac)
    cuts = (
        (slice(2, None), slice(1, -1)),
        (slice(None, -2), slice(1, -1)),
        (slice(1, -1), slice(2, None)),
        (slice(1, -1), slice(None, -2)),
    )
    spread_density = interior(density_now)
    spread_carried = interior(carried)
    spread_moment = interior(moment_two)
    for row_cut, col_cut in cuts:
        weight = (
            0.5 * (reach_mid + reach_map[row_cut, col_cut]) * land_mid * land_frac[row_cut, col_cut]
        )
        spread_density = spread_density + weight * (
            density_now[row_cut, col_cut] - interior(density_now)
        )
        spread_carried = spread_carried + weight * (carried[row_cut, col_cut] - interior(carried))
        spread_moment = spread_moment + weight * (
            moment_two[row_cut, col_cut] - interior(moment_two)
        )
    trait_mid = interior(trait_now)
    variance_mid = interior(variance_now)
    denominator = spread_density + PRIOR_WEIGHT
    trait_spread = (spread_carried + PRIOR_WEIGHT * trait_mid) / denominator
    second_spread = (
        spread_moment + PRIOR_WEIGHT * (variance_mid + trait_mid * trait_mid)
    ) / denominator
    variance_spread = second_spread - trait_spread * trait_spread
    offset = trait_spread - interior(optimum_map)
    growth = land_mid * (
        GROWTH_RATE * (1.0 - spread_density) - 0.5 * selection * (offset * offset + variance_spread)
    )
    density_new = spread_density * jnp.exp(growth)
    response = selection * variance_spread
    trait_new = trait_spread - response * offset / (1.0 + response)
    variance_new = variance_spread / (1.0 + response) + MUTATION_INPUT
    return jnp.stack([density_new, trait_new, variance_new])


def adam_update(raw_maps, first_now, second_now, gradient):
    first_new = BETA_FIRST * first_now + (1.0 - BETA_FIRST) * gradient
    second_new = BETA_SECOND * second_now + (1.0 - BETA_SECOND) * gradient * gradient
    first_hat = first_new / (1.0 - BETA_FIRST**ADAM_STEP)
    second_hat = second_new / (1.0 - BETA_SECOND**ADAM_STEP)
    maps_new = raw_maps - LEARN_RATE * first_hat / (jnp.sqrt(second_hat) + ADAM_EPS)
    return (maps_new, first_new, second_new)


def state_halo(fields):
    return extended(fields, (("lx", 1), ("ly", 2)), 2)


def adjoint_halo(adjoint_now):
    return extended(adjoint_now, (("lx", 1), ("ly", 2)), 1)


def shards(
    density,
    trait,
    variance,
    optimum,
    observed,
    obs_step,
    land_code,
    maps,
    first_moment,
    second_moment,
):
    land_frac = land_code.astype(jnp.float32)
    statics = jnp.concatenate([maps, optimum, land_frac[None]], axis=0)
    fields = jnp.concatenate([density, trait, variance], axis=0)
    padded_states = []
    later_states = []
    static_wide = extended(statics, (("lx", 1), ("ly", 2)), 2)
    raw_near = interior(static_wide[0:2])
    optimum_near = interior(static_wide[2])
    land_near = interior(static_wide[3])
    for step_index in range(STEPS):
        padded = state_halo(fields)
        padded_states.append(padded)
        fields = advance(interior(padded), raw_near, optimum_near, land_near)
        later_states.append(fields)
    raw_wide = static_wide[0:2]
    optimum_wide = static_wide[2]
    land_wide = static_wide[3]
    chosen_rows = obs_step[0]

    def forward_wide(field_block, raw_block):
        return advance(field_block, raw_block, optimum_wide, land_wide)

    adjoint_now = jnp.zeros_like(later_states[-1])
    gradient = jnp.zeros(maps.shape, jnp.float32)
    for step_index in reversed(range(STEPS)):
        chosen = (chosen_rows == step_index + 1).astype(jnp.float32)[:, None]
        source = (
            2.0 * LOSS_WEIGHT * chosen * land_frac * (later_states[step_index][0] - observed[0])
        )
        blank = jnp.zeros_like(source)
        adjoint_now = adjoint_now + jnp.stack([source, blank, blank])
        adjoint_wide = adjoint_halo(adjoint_now)
        outputs, pullback = jax.vjp(forward_wide, padded_states[step_index], raw_wide)
        cot_fields, cot_maps = pullback(adjoint_wide)
        adjoint_now = cot_fields[:, 2:-2, 2:-2]
        gradient = gradient + cot_maps[:, 2:-2, 2:-2]
    share = lax.psum_scatter(gradient, "scen", scatter_dimension=1, tiled=True)
    share_rows = share.shape[1]
    row_start = lax.axis_index("scen") * share_rows
    maps_own = lax.dynamic_slice_in_dim(maps, row_start, share_rows, 1)
    first_own = lax.dynamic_slice_in_dim(first_moment, row_start, share_rows, 1)
    second_own = lax.dynamic_slice_in_dim(second_moment, row_start, share_rows, 1)
    maps_part, first_part, second_part = adam_update(maps_own, first_own, second_own, share)
    new_maps, new_first, new_second = (
        lax.all_gather(maps_part, "scen", axis=1, tiled=True),
        lax.all_gather(first_part, "scen", axis=1, tiled=True),
        lax.all_gather(second_part, "scen", axis=1, tiled=True),
    )
    return (new_maps, new_first, new_second)


def solution(mesh):
    in_specs = (
        P("scen", "lx", "ly"),
        P("scen", "lx", "ly"),
        P("scen", "lx", "ly"),
        P("scen", "lx", "ly"),
        P("scen", "lx", "ly"),
        P("scen", "lx"),
        P("lx", "ly"),
        P(None, "lx", "ly"),
        P(None, "lx", "ly"),
        P(None, "lx", "ly"),
    )
    out_specs = (P(None, "lx", "ly"), P(None, "lx", "ly"), P(None, "lx", "ly"))
    return jax.shard_map(shards, mesh=mesh, in_specs=in_specs, out_specs=out_specs, check_vma=False)
```

profile of v0, /device:TPU:32, one launch (start us, length us, event | category | flops | bytes accessed | tf_op | source)
XLA Modules:
  0.0 307.5 jit_solution(4712670643608340800)
XLA Ops:
  10.3 1.9 collective-permute-start
  12.2 3.6 %collective-permute-start.1 = (f32[3,2,512]{2,1,0:T(2,128)S(1)}, f32[3,2,512]{2,1,0:T(2,128)S(1)}, u32[]{:S(2)}, u32[]{:S(2)}) collective-permute-start(f32[3,2,512]{2,1,0:T(2,128)S(1)} %get-tuple-element.120), channel_id=1, source_target_pairs={{4,0},{8,4},{12,8},{5,1},{9,5},{13,9},{6,2},{10,6},{14,10},{7,3},{... | collective-permute-start | bytes 36872 | tf_op jit(solution)/shard_map/ppermute | solution.py:27
  15.9 1.9 collective-permute-start.4
  17.9 3.6 %collective-permute-start.5 = (f32[4,2,512]{2,1,0:T(2,128)S(1)}, f32[4,2,512]{2,1,0:T(2,128)S(1)}, u32[]{:S(2)}, u32[]{:S(2)}) collective-permute-start(f32[4,2,512]{2,1,0:T(2,128)S(1)} %get-tuple-element.86), channel_id=1, source_target_pairs={{4,0},{8,4},{12,8},{5,1},{9,5},{13,9},{6,2},{10,6},{14,10},{7,3},{... | collective-permute-start | bytes 49160 | tf_op jit(solution)/shard_map/ppermute | solution.py:27
  21.7 5.2 %collective-permute-start.2 = (f32[3,132,2]{2,1,0:T(8,128)S(1)}, f32[3,132,2]{2,1,0:T(8,128)S(1)}, u32[]{:S(2)}, u32[]{:S(2)}) collective-permute-start(f32[3,132,2]{2,1,0:T(8,128)S(1)} %get-tuple-element.109), channel_id=1, source_target_pairs={{0,1},{1,2},{2,3},{4,5},{5,6},{6,7},{8,9},{9,10},{10,11},{12,13},{... | collective-permute-start | bytes 9512 | tf_op jit(solution)/shard_map/ppermute | solution.py:24
  28.2 6.2 %collective-permute-done.2 = f32[3,132,2]{2,1,0:T(8,128)S(1)} collective-permute-done((f32[3,132,2]{2,1,0:T(8,128)S(1)}, f32[3,132,2]{2,1,0:T(8,128)S(1)}, u32[]{:S(2)}, u32[]{:S(2)}) %collective-permute-start.2) | collective-permute-done | bytes 3200 | tf_op jit(solution)/shard_map/ppermute | solution.py:24
  34.4 3.0 collective-permute-done.3
  38.4 8.1 %collective-permute-start.6 = (f32[4,132,2]{2,1,0:T(8,128)S(1)}, f32[4,132,2]{2,1,0:T(8,128)S(1)}, u32[]{:S(2)}, u32[]{:S(2)}) collective-permute-start(f32[4,132,2]{2,1,0:T(8,128)S(1)} %get-tuple-element.83), channel_id=1, source_target_pairs={{0,1},{1,2},{2,3},{4,5},{5,6},{6,7},{8,9},{9,10},{10,11},{12,13},{... | collective-permute-start | bytes 12680 | tf_op jit(solution)/shard_map/ppermute | solution.py:24
  48.1 7.9 %collective-permute-done.6 = f32[4,132,2]{2,1,0:T(8,128)S(1)} collective-permute-done((f32[4,132,2]{2,1,0:T(8,128)S(1)}, f32[4,132,2]{2,1,0:T(8,128)S(1)}, u32[]{:S(2)}, u32[]{:S(2)}) %collective-permute-start.6) | collective-permute-done | bytes 4256 | tf_op jit(solution)/shard_map/ppermute | solution.py:24
  56.0 5.7 %collective-permute-done.7 = f32[4,132,2]{2,1,0:T(8,128)S(1)} collective-permute-done((f32[4,132,2]{2,1,0:T(8,128)S(1)}, f32[4,132,2]{2,1,0:T(8,128)S(1)}, u32[]{:S(2)}, u32[]{:S(2)}) %collective-permute-start.7) | collective-permute-done | bytes 4256 | tf_op jit(solution)/shard_map/ppermute | solution.py:27
  65.1 1.9 collective-permute-start.8
  67.1 3.6 %collective-permute-start.9 = (f32[3,2,512]{2,1,0:T(2,128)S(1)}, f32[3,2,512]{2,1,0:T(2,128)S(1)}, u32[]{:S(2)}, u32[]{:S(2)}) collective-permute-start(f32[3,2,512]{2,1,0:T(2,128)S(1)} %get-tuple-element.118), channel_id=1, source_target_pairs={{4,0},{8,4},{12,8},{5,1},{9,5},{13,9},{6,2},{10,6},{14,10},{7,3},{... | collective-permute-start | bytes 36872 | tf_op jit(solution)/shard_map/ppermute | solution.py:27
  72.2 3.1 collective-permute-start.10
  76.7 5.9 %collective-permute-done.10 = f32[3,132,2]{2,1,0:T(8,128)S(1)} collective-permute-done((f32[3,132,2]{2,1,0:T(8,128)S(1)}, f32[3,132,2]{2,1,0:T(8,128)S(1)}, u32[]{:S(2)}, u32[]{:S(2)}) %collective-permute-start.10) | collective-permute-done | bytes 3200 | tf_op jit(solution)/shard_map/ppermute | solution.py:24
  82.6 5.3 %collective-permute-done.11 = f32[3,132,2]{2,1,0:T(8,128)S(1)} collective-permute-done((f32[3,132,2]{2,1,0:T(8,128)S(1)}, f32[3,132,2]{2,1,0:T(8,128)S(1)}, u32[]{:S(2)}, u32[]{:S(2)}) %collective-permute-start.11) | collective-permute-done | bytes 3200 | tf_op jit(solution)/shard_map/ppermute | solution.py:27
  92.4 3.6 %collective-permute-start.13 = (f32[3,1,512]{2,1,0:T(1,128)S(1)}, f32[3,1,512]{2,1,0:T(1,128)S(1)}, u32[]{:S(2)}, u32[]{:S(2)}) collective-permute-start(f32[3,1,512]{2,1,0:T(1,128)S(1)} %get-tuple-element.148), channel_id=1, source_target_pairs={{4,0},{8,4},{12,8},{5,1},{9,5},{13,9},{6,2},{10,6},{14,10},{7,3},{... | collective-permute-start | bytes 18440 | tf_op jit(solution)/shard_map/ppermute | solution.py:27
  97.5 3.2 %collective-permute-start.14 = (f32[3,130,1]{2,1,0:T(8,128)S(1)}, f32[3,130,1]{2,1,0:T(8,128)S(1)}, u32[]{:S(2)}, u32[]{:S(2)}) collective-permute-start(f32[3,130,1]{2,1,0:T(8,128)S(1)} %get-tuple-element.113), channel_id=1, source_target_pairs={{0,1},{1,2},{2,3},{4,5},{5,6},{6,7},{8,9},{9,10},{10,11},{12,13},{... | collective-permute-start | bytes 4688 | tf_op jit(solution)/shard_map/ppermute | solution.py:24
  102.3 5.8 %collective-permute-done.14 = f32[3,130,1]{2,1,0:T(8,128)S(1)} collective-permute-done((f32[3,130,1]{2,1,0:T(8,128)S(1)}, f32[3,130,1]{2,1,0:T(8,128)S(1)}, u32[]{:S(2)}, u32[]{:S(2)}) %collective-permute-start.14) | collective-permute-done | bytes 1592 | tf_op jit(solution)/shard_map/ppermute | solution.py:24
  108.0 5.3 %collective-permute-done.15 = f32[3,130,1]{2,1,0:T(8,128)S(1)} collective-permute-done((f32[3,130,1]{2,1,0:T(8,128)S(1)}, f32[3,130,1]{2,1,0:T(8,128)S(1)}, u32[]{:S(2)}, u32[]{:S(2)}) %collective-permute-start.15) | collective-permute-done | bytes 1592 | tf_op jit(solution)/shard_map/ppermute | solution.py:27
  113.8 2.4 add_multiply_fusion.2
  116.2 2.3 add_add_fusion.7
  122.7 1.9 collective-permute-start.16
  124.7 3.6 %collective-permute-start.17 = (f32[3,1,512]{2,1,0:T(1,128)S(1)}, f32[3,1,512]{2,1,0:T(1,128)S(1)}, u32[]{:S(2)}, u32[]{:S(2)}) collective-permute-start(f32[3,1,512]{2,1,0:T(1,128)S(1)} %get-tuple-element.116), channel_id=1, source_target_pairs={{4,0},{8,4},{12,8},{5,1},{9,5},{13,9},{6,2},{10,6},{14,10},{7,3},{... | collective-permute-start | bytes 18440 | tf_op jit(solution)/shard_map/ppermute | solution.py:27
  129.8 3.1 %collective-permute-start.18 = (f32[3,130,1]{2,1,0:T(8,128)S(1)}, f32[3,130,1]{2,1,0:T(8,128)S(1)}, u32[]{:S(2)}, u32[]{:S(2)}) collective-permute-start(f32[3,130,1]{2,1,0:T(8,128)S(1)} %get-tuple-element.111), channel_id=1, source_target_pairs={{0,1},{1,2},{2,3},{4,5},{5,6},{6,7},{8,9},{9,10},{10,11},{12,13},{... | collective-permute-start | bytes 4688 | tf_op jit(solution)/shard_map/ppermute | solution.py:24
  134.6 5.7 %collective-permute-done.18 = f32[3,130,1]{2,1,0:T(8,128)S(1)} collective-permute-done((f32[3,130,1]{2,1,0:T(8,128)S(1)}, f32[3,130,1]{2,1,0:T(8,128)S(1)}, u32[]{:S(2)}, u32[]{:S(2)}) %collective-permute-start.18) | collective-permute-done | bytes 1592 | tf_op jit(solution)/shard_map/ppermute | solution.py:24
  140.2 5.3 %collective-permute-done.19 = f32[3,130,1]{2,1,0:T(8,128)S(1)} collective-permute-done((f32[3,130,1]{2,1,0:T(8,128)S(1)}, f32[3,130,1]{2,1,0:T(8,128)S(1)}, u32[]{:S(2)}, u32[]{:S(2)}) %collective-permute-start.19) | collective-permute-done | bytes 1592 | tf_op jit(solution)/shard_map/ppermute | solution.py:27
  146.0 2.0 add_multiply_fusion
  149.1 2.3 add_add_fusion.5
  153.4 75.6 %reduce-scatter.2.cloned.1.call-done = f32[2,8,512]{2,1,0:T(8,128)} async-done(((f32[2,128,512]{2,1,0:T(8,128)}), f32[2,8,512]{2,1,0:T(8,128)}) %reduce-scatter.2.cloned.1.call-update) | async-done | bytes 32784 | tf_op jit(solution)/shard_map/reduce_scatter | solution.py:148
  229.9 23.3 %all_gather.9 = f32[2,128,512]{2,1,0:T(8,128)S(1)} all-gather(f32[2,8,512]{2,1,0:T(8,128)S(1)} %get-tuple-element.7), channel_id=1, replica_groups=mesh['scen'=16,'lx'=4,'ly'=4] {'scen'}, dimensions={1}, use_global_device_ids=true | all-gather | bytes 557056 | tf_op jit(solution)/shard_map/all_gather | solution.py:156
  253.2 22.1 %all_gather.10 = f32[2,128,512]{2,1,0:T(8,128)S(1)} all-gather(f32[2,8,512]{2,1,0:T(8,128)S(1)} %get-tuple-element.8), channel_id=1, replica_groups=mesh['scen'=16,'lx'=4,'ly'=4] {'scen'}, dimensions={1}, use_global_device_ids=true | all-gather | bytes 557056 | tf_op jit(solution)/shard_map/all_gather | solution.py:157
  275.3 23.0 %all_gather.11 = f32[2,128,512]{2,1,0:T(8,128)S(1)} all-gather(f32[2,8,512]{2,1,0:T(8,128)S(1)} %get-tuple-element.9), channel_id=1, replica_groups=mesh['scen'=16,'lx'=4,'ly'=4] {'scen'}, dimensions={1}, use_global_device_ids=true | all-gather | bytes 557056 | tf_op jit(solution)/shard_map/all_gather | solution.py:158
  (77 shorter events, 35.2 us)
Async XLA Ops:
  7.2 8.7 %copy-start.1 = (s32[128,512]{1,0:T(8,128)S(1)}, s32[128,512]{1,0:T(8,128)}, u32[]{:S(2)}) copy-start(s32[128,512]{1,0:T(8,128)} %param.17) | copy-start | bytes 786436
  7.2 8.7 %copy-start.2 = (f32[1,128,512]{2,1,0:T(8,128)S(1)}, f32[1,128,512]{2,1,0:T(8,128)}, u32[]{:S(2)}) copy-start(f32[1,128,512]{2,1,0:T(8,128)} %param.14) | copy-start | bytes 786436
  7.2 8.7 %copy-start = (f32[2,128,512]{2,1,0:T(8,128)S(1)}, f32[2,128,512]{2,1,0:T(8,128)}, u32[]{:S(2)}) copy-start(f32[2,128,512]{2,1,0:T(8,128)} %param.18) | copy-start | bytes 1572868
  7.2 221.9 %reduce-scatter.2.cloned.1.call-start = ((), (), s32[]{:S(2)}) async-start(), calls=%async_computation.1 | async-start | bytes 557056 | tf_op jit(solution)/shard_map/reduce_scatter | solution.py:148
  10.3 11.3 %collective-permute-start = (f32[3,2,512]{2,1,0:T(2,128)S(1)}, f32[3,2,512]{2,1,0:T(2,128)S(1)}, u32[]{:S(2)}, u32[]{:S(2)}) collective-permute-start(f32[3,2,512]{2,1,0:T(2,128)S(1)} %get-tuple-element.119), channel_id=1, source_target_pairs={{0,4},{4,8},{8,12},{1,5},{5,9},{9,13},{2,6},{6,10},{10,14},{3,7},{... | collective-permute-start | bytes 36872 | tf_op jit(solution)/shard_map/ppermute | solution.py:24
  12.2 16.0 %copy-start.4 = (s32[1,128]{1,0:T(1,128)S(1)}, s32[1,128]{1,0:T(1,128)}, u32[]{:S(2)}) copy-start(s32[1,128]{1,0:T(1,128)} %param.16) | copy-start | bytes 1540
  12.2 9.3 %collective-permute-start.1 = (f32[3,2,512]{2,1,0:T(2,128)S(1)}, f32[3,2,512]{2,1,0:T(2,128)S(1)}, u32[]{:S(2)}, u32[]{:S(2)}) collective-permute-start(f32[3,2,512]{2,1,0:T(2,128)S(1)} %get-tuple-element.120), channel_id=1, source_target_pairs={{4,0},{8,4},{12,8},{5,1},{9,5},{13,9},{6,2},{10,6},{14,10},{7,3},{... | collective-permute-start | bytes 36872 | tf_op jit(solution)/shard_map/ppermute | solution.py:27
  15.9 22.3 %collective-permute-start.4 = (f32[4,2,512]{2,1,0:T(2,128)S(1)}, f32[4,2,512]{2,1,0:T(2,128)S(1)}, u32[]{:S(2)}, u32[]{:S(2)}) collective-permute-start(f32[4,2,512]{2,1,0:T(2,128)S(1)} %get-tuple-element.85), channel_id=1, source_target_pairs={{0,4},{4,8},{8,12},{1,5},{5,9},{9,13},{2,6},{6,10},{10,14},{3,7},{... | collective-permute-start | bytes 49160 | tf_op jit(solution)/shard_map/ppermute | solution.py:24
  17.9 20.3 %collective-permute-start.5 = (f32[4,2,512]{2,1,0:T(2,128)S(1)}, f32[4,2,512]{2,1,0:T(2,128)S(1)}, u32[]{:S(2)}, u32[]{:S(2)}) collective-permute-start(f32[4,2,512]{2,1,0:T(2,128)S(1)} %get-tuple-element.86), channel_id=1, source_target_pairs={{4,0},{8,4},{12,8},{5,1},{9,5},{13,9},{6,2},{10,6},{14,10},{7,3},{... | collective-permute-start | bytes 49160 | tf_op jit(solution)/shard_map/ppermute | solution.py:27
  21.7 12.7 %collective-permute-start.2 = (f32[3,132,2]{2,1,0:T(8,128)S(1)}, f32[3,132,2]{2,1,0:T(8,128)S(1)}, u32[]{:S(2)}, u32[]{:S(2)}) collective-permute-start(f32[3,132,2]{2,1,0:T(8,128)S(1)} %get-tuple-element.109), channel_id=1, source_target_pairs={{0,1},{1,2},{2,3},{4,5},{5,6},{6,7},{8,9},{9,10},{10,11},{12,13},{... | collective-permute-start | bytes 9512 | tf_op jit(solution)/shard_map/ppermute | solution.py:24
  26.9 10.5 %collective-permute-start.3 = (f32[3,132,2]{2,1,0:T(8,128)S(1)}, f32[3,132,2]{2,1,0:T(8,128)S(1)}, u32[]{:S(2)}, u32[]{:S(2)}) collective-permute-start(f32[3,132,2]{2,1,0:T(8,128)S(1)} %get-tuple-element.110), channel_id=1, source_target_pairs={{1,0},{2,1},{3,2},{5,4},{6,5},{7,6},{9,8},{10,9},{11,10},{13,12},{... | collective-permute-start | bytes 9512 | tf_op jit(solution)/shard_map/ppermute | solution.py:27
  38.4 17.6 %collective-permute-start.6 = (f32[4,132,2]{2,1,0:T(8,128)S(1)}, f32[4,132,2]{2,1,0:T(8,128)S(1)}, u32[]{:S(2)}, u32[]{:S(2)}) collective-permute-start(f32[4,132,2]{2,1,0:T(8,128)S(1)} %get-tuple-element.83), channel_id=1, source_target_pairs={{0,1},{1,2},{2,3},{4,5},{5,6},{6,7},{8,9},{9,10},{10,11},{12,13},{... | collective-permute-start | bytes 12680 | tf_op jit(solution)/shard_map/ppermute | solution.py:24
  46.5 15.3 %collective-permute-start.7 = (f32[4,132,2]{2,1,0:T(8,128)S(1)}, f32[4,132,2]{2,1,0:T(8,128)S(1)}, u32[]{:S(2)}, u32[]{:S(2)}) collective-permute-start(f32[4,132,2]{2,1,0:T(8,128)S(1)} %get-tuple-element.84), channel_id=1, source_target_pairs={{1,0},{2,1},{3,2},{5,4},{6,5},{7,6},{9,8},{10,9},{11,10},{13,12},{... | collective-permute-start | bytes 12680 | tf_op jit(solution)/shard_map/ppermute | solution.py:27
  62.7 1.0 copy-start.3
  65.1 5.6 %collective-permute-start.8 = (f32[3,2,512]{2,1,0:T(2,128)S(1)}, f32[3,2,512]{2,1,0:T(2,128)S(1)}, u32[]{:S(2)}, u32[]{:S(2)}) collective-permute-start(f32[3,2,512]{2,1,0:T(2,128)S(1)} %get-tuple-element.117), channel_id=1, source_target_pairs={{0,4},{4,8},{8,12},{1,5},{5,9},{9,13},{2,6},{6,10},{10,14},{3,7},{... | collective-permute-start | bytes 36872 | tf_op jit(solution)/shard_map/ppermute | solution.py:24
  67.1 5.0 %collective-permute-start.9 = (f32[3,2,512]{2,1,0:T(2,128)S(1)}, f32[3,2,512]{2,1,0:T(2,128)S(1)}, u32[]{:S(2)}, u32[]{:S(2)}) collective-permute-start(f32[3,2,512]{2,1,0:T(2,128)S(1)} %get-tuple-element.118), channel_id=1, source_target_pairs={{4,0},{8,4},{12,8},{5,1},{9,5},{13,9},{6,2},{10,6},{14,10},{7,3},{... | collective-permute-start | bytes 36872 | tf_op jit(solution)/shard_map/ppermute | solution.py:27
  72.2 10.4 %collective-permute-start.10 = (f32[3,132,2]{2,1,0:T(8,128)S(1)}, f32[3,132,2]{2,1,0:T(8,128)S(1)}, u32[]{:S(2)}, u32[]{:S(2)}) collective-permute-start(f32[3,132,2]{2,1,0:T(8,128)S(1)} %get-tuple-element.107), channel_id=1, source_target_pairs={{0,1},{1,2},{2,3},{4,5},{5,6},{6,7},{8,9},{9,10},{10,11},{12,13},{... | collective-permute-start | bytes 9512 | tf_op jit(solution)/shard_map/ppermute | solution.py:24
  75.3 12.6 %collective-permute-start.11 = (f32[3,132,2]{2,1,0:T(8,128)S(1)}, f32[3,132,2]{2,1,0:T(8,128)S(1)}, u32[]{:S(2)}, u32[]{:S(2)}) collective-permute-start(f32[3,132,2]{2,1,0:T(8,128)S(1)} %get-tuple-element.108), channel_id=1, source_target_pairs={{1,0},{2,1},{3,2},{5,4},{6,5},{7,6},{9,8},{10,9},{11,10},{13,12},{... | collective-permute-start | bytes 9512 | tf_op jit(solution)/shard_map/ppermute | solution.py:27
  90.5 5.8 %collective-permute-start.12 = (f32[3,1,512]{2,1,0:T(1,128)S(1)}, f32[3,1,512]{2,1,0:T(1,128)S(1)}, u32[]{:S(2)}, u32[]{:S(2)}) collective-permute-start(f32[3,1,512]{2,1,0:T(1,128)S(1)} %get-tuple-element.147), channel_id=1, source_target_pairs={{0,4},{4,8},{8,12},{1,5},{5,9},{9,13},{2,6},{6,10},{10,14},{3,7},{... | collective-permute-start | bytes 18440 | tf_op jit(solution)/shard_map/ppermute | solution.py:24
  92.4 5.0 %collective-permute-start.13 = (f32[3,1,512]{2,1,0:T(1,128)S(1)}, f32[3,1,512]{2,1,0:T(1,128)S(1)}, u32[]{:S(2)}, u32[]{:S(2)}) collective-permute-start(f32[3,1,512]{2,1,0:T(1,128)S(1)} %get-tuple-element.148), channel_id=1, source_target_pairs={{4,0},{8,4},{12,8},{5,1},{9,5},{13,9},{6,2},{10,6},{14,10},{7,3},{... | collective-permute-start | bytes 18440 | tf_op jit(solution)/shard_map/ppermute | solution.py:27
  97.5 10.5 %collective-permute-start.14 = (f32[3,130,1]{2,1,0:T(8,128)S(1)}, f32[3,130,1]{2,1,0:T(8,128)S(1)}, u32[]{:S(2)}, u32[]{:S(2)}) collective-permute-start(f32[3,130,1]{2,1,0:T(8,128)S(1)} %get-tuple-element.113), channel_id=1, source_target_pairs={{0,1},{1,2},{2,3},{4,5},{5,6},{6,7},{8,9},{9,10},{10,11},{12,13},{... | collective-permute-start | bytes 4688 | tf_op jit(solution)/shard_map/ppermute | solution.py:24
  100.7 12.7 %collective-permute-start.15 = (f32[3,130,1]{2,1,0:T(8,128)S(1)}, f32[3,130,1]{2,1,0:T(8,128)S(1)}, u32[]{:S(2)}, u32[]{:S(2)}) collective-permute-start(f32[3,130,1]{2,1,0:T(8,128)S(1)} %get-tuple-element.114), channel_id=1, source_target_pairs={{1,0},{2,1},{3,2},{5,4},{6,5},{7,6},{9,8},{10,9},{11,10},{13,12},{... | collective-permute-start | bytes 4688 | tf_op jit(solution)/shard_map/ppermute | solution.py:27
  122.7 5.7 %collective-permute-start.16 = (f32[3,1,512]{2,1,0:T(1,128)S(1)}, f32[3,1,512]{2,1,0:T(1,128)S(1)}, u32[]{:S(2)}, u32[]{:S(2)}) collective-permute-start(f32[3,1,512]{2,1,0:T(1,128)S(1)} %get-tuple-element.115), channel_id=1, source_target_pairs={{0,4},{4,8},{8,12},{1,5},{5,9},{9,13},{2,6},{6,10},{10,14},{3,7},{... | collective-permute-start | bytes 18440 | tf_op jit(solution)/shard_map/ppermute | solution.py:24
  124.7 5.0 %collective-permute-start.17 = (f32[3,1,512]{2,1,0:T(1,128)S(1)}, f32[3,1,512]{2,1,0:T(1,128)S(1)}, u32[]{:S(2)}, u32[]{:S(2)}) collective-permute-start(f32[3,1,512]{2,1,0:T(1,128)S(1)} %get-tuple-element.116), channel_id=1, source_target_pairs={{4,0},{8,4},{12,8},{5,1},{9,5},{13,9},{6,2},{10,6},{14,10},{7,3},{... | collective-permute-start | bytes 18440 | tf_op jit(solution)/shard_map/ppermute | solution.py:27
  129.8 10.5 %collective-permute-start.18 = (f32[3,130,1]{2,1,0:T(8,128)S(1)}, f32[3,130,1]{2,1,0:T(8,128)S(1)}, u32[]{:S(2)}, u32[]{:S(2)}) collective-permute-start(f32[3,130,1]{2,1,0:T(8,128)S(1)} %get-tuple-element.111), channel_id=1, source_target_pairs={{0,1},{1,2},{2,3},{4,5},{5,6},{6,7},{8,9},{9,10},{10,11},{12,13},{... | collective-permute-start | bytes 4688 | tf_op jit(solution)/shard_map/ppermute | solution.py:24
  132.9 12.7 %collective-permute-start.19 = (f32[3,130,1]{2,1,0:T(8,128)S(1)}, f32[3,130,1]{2,1,0:T(8,128)S(1)}, u32[]{:S(2)}, u32[]{:S(2)}) collective-permute-start(f32[3,130,1]{2,1,0:T(8,128)S(1)} %get-tuple-element.112), channel_id=1, source_target_pairs={{1,0},{2,1},{3,2},{5,4},{6,5},{7,6},{9,8},{10,9},{11,10},{13,12},{... | collective-permute-start | bytes 4688 | tf_op jit(solution)/shard_map/ppermute | solution.py:27
Sparse Core Ops, SparseCore 0:
  153.5 75.4 reduce-scatter.1
where the time goes:
time: 308 us
  waiting for transfers between devices  135 us (44%)
  blocking collectives  68.4 us (22%)
  starting transfers between devices  57.4 us (19%)
  other arithmetic  25 us (8%)
  between operations  14.6 us (5%)
  local copies, waits for them, and re-layouts  6.75 us (2%)
    reduce_scatter x1, waiting for transfers between devices, shards(): share = lax.psum_scatter(gradient, 'scen', scatter_dimension=1, tiled=True)  75.6 us
    ppermute x10, starting transfers between devices, extended(): lax.ppermute(lax.slice_in_dim(block, block.shape[dim] - width, None, axis...  32.2 us
    ppermute x10, waiting for transfers between devices, extended(): lax.ppermute(lax.slice_in_dim(block, block.shape[dim] - width, None, axis...  31.4 us
    ppermute x10, waiting for transfers between devices, extended(): lax.ppermute(lax.slice_in_dim(block, 0, width, axis=dim), axis, backward)  28.4 us
    ppermute x10, starting transfers between devices, extended(): lax.ppermute(lax.slice_in_dim(block, 0, width, axis=dim), axis, backward)  25.1 us
    all_gather x1, blocking collectives, shards(): lax.all_gather(maps_part, 'scen', axis=1, tiled=True)  23.3 us
    all_gather x1, blocking collectives, shards(): lax.all_gather(second_part, 'scen', axis=1, tiled=True)  23 us
    all_gather x1, blocking collectives, shards(): lax.all_gather(first_part, 'scen', axis=1, tiled=True)  22.1 us
  transfers between devices with their start and end apart: 21, of which 14 were waited for; matrix products, arithmetic and copies ran while one was open for 1% of the time, Pallas kernels for 0%

commit v1 on v0

--- a/solution.py
+++ b/solution.py
@@ -153,7 +153,9 @@
     second_own = lax.dynamic_slice_in_dim(second_moment, row_start, share_rows, 1)
     maps_part, first_part, second_part = adam_update(maps_own, first_own, second_own, share)
     new_maps, new_first, new_second = (
-        lax.all_gather(maps_part, "scen", axis=1, tiled=True),
+        jnp.concatenate(
+            lax.all_to_all(jnp.stack([maps_part] * lax.axis_size("scen")), "scen", 0, 0), axis=1
+        ),
         lax.all_gather(first_part, "scen", axis=1, tiled=True),
         lax.all_gather(second_part, "scen", axis=1, tiled=True),
     )

time: 308 us -> 294 us (0.955)
  blocking collectives: 68.4 us -> 48 us
  starting transfers between devices: 57.4 us -> 62.3 us
    all_gather x1 -> x0, blocking collectives: 23.3 us -> none  [shards(): lax.all_gather(maps_part, 'scen', axis=1, tiled=True)]
    all_to_all x0 -> x1, starting transfers between devices: none -> 4.99 us  [shards(): lax.all_to_all(jnp.stack([maps_part] * lax.axis_size('scen')), 'scen', 0, 0)]
  transfers between devices with their start and end apart: 21 -> 22, of which waited for: 14 -> 14; matrix products, arithmetic and copies ran while one was open for 1% -> 1% of each run, Pallas kernels for 0% -> 0%
where the time goes in v1:
time: 294 us; the launch traced here: 293 us
  waiting for transfers between devices  135 us (46%)
  starting transfers between devices  62.3 us (21%)
  blocking collectives  48 us (16%)
  other arithmetic  25 us (9%)
  between operations  14.6 us (5%)
  local copies, waits for them, and re-layouts  7.64 us (3%)
    reduce_scatter x1, waiting for transfers between devices, shards(): share = lax.psum_scatter(gradient, 'scen', scatter_dimension=1, tiled=True)  75.6 us
    ppermute x10, starting transfers between devices, extended(): lax.ppermute(lax.slice_in_dim(block, block.shape[dim] - width, None, axis...  32.2 us
    ppermute x10, waiting for transfers between devices, extended(): lax.ppermute(lax.slice_in_dim(block, block.shape[dim] - width, None, axis...  31.4 us
    ppermute x10, waiting for transfers between devices, extended(): lax.ppermute(lax.slice_in_dim(block, 0, width, axis=dim), axis, backward)  28.4 us
    all_gather x1, blocking collectives, shards(): lax.all_gather(first_part, 'scen', axis=1, tiled=True)  25.2 us
    ppermute x10, starting transfers between devices, extended(): lax.ppermute(lax.slice_in_dim(block, 0, width, axis=dim), axis, backward)  25.1 us
    all_gather x1, blocking collectives, shards(): lax.all_gather(second_part, 'scen', axis=1, tiled=True)  22.9 us
  transfers between devices with their start and end apart: 22, of which 14 were waited for; matrix products, arithmetic and copies ran while one was open for 1% of the time, Pallas kernels for 0%

profile of v1, /device:TPU:32, one launch (start us, length us, event | category | flops | bytes accessed | tf_op | source)
XLA Modules:
  0.0 293.0 jit_solution(4613335232087056575)
XLA Ops:
  10.3 1.9 collective-permute-start
  12.2 3.6 %collective-permute-start.1 = (f32[3,2,512]{2,1,0:T(2,128)S(1)}, f32[3,2,512]{2,1,0:T(2,128)S(1)}, u32[]{:S(2)}, u32[]{:S(2)}) collective-permute-start(f32[3,2,512]{2,1,0:T(2,128)S(1)} %get-tuple-element.120), channel_id=1, source_target_pairs={{4,0},{8,4},{12,8},{5,1},{9,5},{13,9},{6,2},{10,6},{14,10},{7,3},{... | collective-permute-start | bytes 36872 | tf_op jit(solution)/shard_map/ppermute | solution.py:27
  15.9 1.9 collective-permute-start.4
  17.9 3.6 %collective-permute-start.5 = (f32[4,2,512]{2,1,0:T(2,128)S(1)}, f32[4,2,512]{2,1,0:T(2,128)S(1)}, u32[]{:S(2)}, u32[]{:S(2)}) collective-permute-start(f32[4,2,512]{2,1,0:T(2,128)S(1)} %get-tuple-element.86), channel_id=1, source_target_pairs={{4,0},{8,4},{12,8},{5,1},{9,5},{13,9},{6,2},{10,6},{14,10},{7,3},{... | collective-permute-start | bytes 49160 | tf_op jit(solution)/shard_map/ppermute | solution.py:27
  21.7 5.2 %collective-permute-start.2 = (f32[3,132,2]{2,1,0:T(8,128)S(1)}, f32[3,132,2]{2,1,0:T(8,128)S(1)}, u32[]{:S(2)}, u32[]{:S(2)}) collective-permute-start(f32[3,132,2]{2,1,0:T(8,128)S(1)} %get-tuple-element.109), channel_id=1, source_target_pairs={{0,1},{1,2},{2,3},{4,5},{5,6},{6,7},{8,9},{9,10},{10,11},{12,13},{... | collective-permute-start | bytes 9512 | tf_op jit(solution)/shard_map/ppermute | solution.py:24
  28.2 6.2 %collective-permute-done.2 = f32[3,132,2]{2,1,0:T(8,128)S(1)} collective-permute-done((f32[3,132,2]{2,1,0:T(8,128)S(1)}, f32[3,132,2]{2,1,0:T(8,128)S(1)}, u32[]{:S(2)}, u32[]{:S(2)}) %collective-permute-start.2) | collective-permute-done | bytes 3200 | tf_op jit(solution)/shard_map/ppermute | solution.py:24
  34.4 3.0 %collective-permute-done.3 = f32[3,132,2]{2,1,0:T(8,128)S(1)} collective-permute-done((f32[3,132,2]{2,1,0:T(8,128)S(1)}, f32[3,132,2]{2,1,0:T(8,128)S(1)}, u32[]{:S(2)}, u32[]{:S(2)}) %collective-permute-start.3) | collective-permute-done | bytes 3200 | tf_op jit(solution)/shard_map/ppermute | solution.py:27
  38.4 8.1 %collective-permute-start.6 = (f32[4,132,2]{2,1,0:T(8,128)S(1)}, f32[4,132,2]{2,1,0:T(8,128)S(1)}, u32[]{:S(2)}, u32[]{:S(2)}) collective-permute-start(f32[4,132,2]{2,1,0:T(8,128)S(1)} %get-tuple-element.83), channel_id=1, source_target_pairs={{0,1},{1,2},{2,3},{4,5},{5,6},{6,7},{8,9},{9,10},{10,11},{12,13},{... | collective-permute-start | bytes 12680 | tf_op jit(solution)/shard_map/ppermute | solution.py:24
  48.1 7.9 %collective-permute-done.6 = f32[4,132,2]{2,1,0:T(8,128)S(1)} collective-permute-done((f32[4,132,2]{2,1,0:T(8,128)S(1)}, f32[4,132,2]{2,1,0:T(8,128)S(1)}, u32[]{:S(2)}, u32[]{:S(2)}) %collective-permute-start.6) | collective-permute-done | bytes 4256 | tf_op jit(solution)/shard_map/ppermute | solution.py:24
  56.0 5.7 %collective-permute-done.7 = f32[4,132,2]{2,1,0:T(8,128)S(1)} collective-permute-done((f32[4,132,2]{2,1,0:T(8,128)S(1)}, f32[4,132,2]{2,1,0:T(8,128)S(1)}, u32[]{:S(2)}, u32[]{:S(2)}) %collective-permute-start.7) | collective-permute-done | bytes 4256 | tf_op jit(solution)/shard_map/ppermute | solution.py:27
  65.1 1.9 collective-permute-start.8
  67.1 3.6 %collective-permute-start.9 = (f32[3,2,512]{2,1,0:T(2,128)S(1)}, f32[3,2,512]{2,1,0:T(2,128)S(1)}, u32[]{:S(2)}, u32[]{:S(2)}) collective-permute-start(f32[3,2,512]{2,1,0:T(2,128)S(1)} %get-tuple-element.118), channel_id=1, source_target_pairs={{4,0},{8,4},{12,8},{5,1},{9,5},{13,9},{6,2},{10,6},{14,10},{7,3},{... | collective-permute-start | bytes 36872 | tf_op jit(solution)/shard_map/ppermute | solution.py:27
  72.3 3.1 %collective-permute-start.10 = (f32[3,132,2]{2,1,0:T(8,128)S(1)}, f32[3,132,2]{2,1,0:T(8,128)S(1)}, u32[]{:S(2)}, u32[]{:S(2)}) collective-permute-start(f32[3,132,2]{2,1,0:T(8,128)S(1)} %get-tuple-element.107), channel_id=1, source_target_pairs={{0,1},{1,2},{2,3},{4,5},{5,6},{6,7},{8,9},{9,10},{10,11},{12,13},{... | collective-permute-start | bytes 9512 | tf_op jit(solution)/shard_map/ppermute | solution.py:24
  76.7 5.9 %collective-permute-done.10 = f32[3,132,2]{2,1,0:T(8,128)S(1)} collective-permute-done((f32[3,132,2]{2,1,0:T(8,128)S(1)}, f32[3,132,2]{2,1,0:T(8,128)S(1)}, u32[]{:S(2)}, u32[]{:S(2)}) %collective-permute-start.10) | collective-permute-done | bytes 3200 | tf_op jit(solution)/shard_map/ppermute | solution.py:24
  82.6 5.3 %collective-permute-done.11 = f32[3,132,2]{2,1,0:T(8,128)S(1)} collective-permute-done((f32[3,132,2]{2,1,0:T(8,128)S(1)}, f32[3,132,2]{2,1,0:T(8,128)S(1)}, u32[]{:S(2)}, u32[]{:S(2)}) %collective-permute-start.11) | collective-permute-done | bytes 3200 | tf_op jit(solution)/shard_map/ppermute | solution.py:27
  92.4 3.6 %collective-permute-start.13 = (f32[3,1,512]{2,1,0:T(1,128)S(1)}, f32[3,1,512]{2,1,0:T(1,128)S(1)}, u32[]{:S(2)}, u32[]{:S(2)}) collective-permute-start(f32[3,1,512]{2,1,0:T(1,128)S(1)} %get-tuple-element.148), channel_id=1, source_target_pairs={{4,0},{8,4},{12,8},{5,1},{9,5},{13,9},{6,2},{10,6},{14,10},{7,3},{... | collective-permute-start | bytes 18440 | tf_op jit(solution)/shard_map/ppermute | solution.py:27
  97.5 3.2 %collective-permute-start.14 = (f32[3,130,1]{2,1,0:T(8,128)S(1)}, f32[3,130,1]{2,1,0:T(8,128)S(1)}, u32[]{:S(2)}, u32[]{:S(2)}) collective-permute-start(f32[3,130,1]{2,1,0:T(8,128)S(1)} %get-tuple-element.113), channel_id=1, source_target_pairs={{0,1},{1,2},{2,3},{4,5},{5,6},{6,7},{8,9},{9,10},{10,11},{12,13},{... | collective-permute-start | bytes 4688 | tf_op jit(solution)/shard_map/ppermute | solution.py:24
  102.3 5.8 %collective-permute-done.14 = f32[3,130,1]{2,1,0:T(8,128)S(1)} collective-permute-done((f32[3,130,1]{2,1,0:T(8,128)S(1)}, f32[3,130,1]{2,1,0:T(8,128)S(1)}, u32[]{:S(2)}, u32[]{:S(2)}) %collective-permute-start.14) | collective-permute-done | bytes 1592 | tf_op jit(solution)/shard_map/ppermute | solution.py:24
  108.1 5.3 %collective-permute-done.15 = f32[3,130,1]{2,1,0:T(8,128)S(1)} collective-permute-done((f32[3,130,1]{2,1,0:T(8,128)S(1)}, f32[3,130,1]{2,1,0:T(8,128)S(1)}, u32[]{:S(2)}, u32[]{:S(2)}) %collective-permute-start.15) | collective-permute-done | bytes 1592 | tf_op jit(solution)/shard_map/ppermute | solution.py:27
  113.8 2.4 add_multiply_fusion.2
  116.2 2.4 add_add_fusion.7
  122.7 1.9 collective-permute-start.16
  124.7 3.6 %collective-permute-start.17 = (f32[3,1,512]{2,1,0:T(1,128)S(1)}, f32[3,1,512]{2,1,0:T(1,128)S(1)}, u32[]{:S(2)}, u32[]{:S(2)}) collective-permute-start(f32[3,1,512]{2,1,0:T(1,128)S(1)} %get-tuple-element.116), channel_id=1, source_target_pairs={{4,0},{8,4},{12,8},{5,1},{9,5},{13,9},{6,2},{10,6},{14,10},{7,3},{... | collective-permute-start | bytes 18440 | tf_op jit(solution)/shard_map/ppermute | solution.py:27
  129.8 3.1 %collective-permute-start.18 = (f32[3,130,1]{2,1,0:T(8,128)S(1)}, f32[3,130,1]{2,1,0:T(8,128)S(1)}, u32[]{:S(2)}, u32[]{:S(2)}) collective-permute-start(f32[3,130,1]{2,1,0:T(8,128)S(1)} %get-tuple-element.111), channel_id=1, source_target_pairs={{0,1},{1,2},{2,3},{4,5},{5,6},{6,7},{8,9},{9,10},{10,11},{12,13},{... | collective-permute-start | bytes 4688 | tf_op jit(solution)/shard_map/ppermute | solution.py:24
  134.6 5.7 %collective-permute-done.18 = f32[3,130,1]{2,1,0:T(8,128)S(1)} collective-permute-done((f32[3,130,1]{2,1,0:T(8,128)S(1)}, f32[3,130,1]{2,1,0:T(8,128)S(1)}, u32[]{:S(2)}, u32[]{:S(2)}) %collective-permute-start.18) | collective-permute-done | bytes 1592 | tf_op jit(solution)/shard_map/ppermute | solution.py:24
  140.3 5.3 %collective-permute-done.19 = f32[3,130,1]{2,1,0:T(8,128)S(1)} collective-permute-done((f32[3,130,1]{2,1,0:T(8,128)S(1)}, f32[3,130,1]{2,1,0:T(8,128)S(1)}, u32[]{:S(2)}, u32[]{:S(2)}) %collective-permute-start.19) | collective-permute-done | bytes 1592 | tf_op jit(solution)/shard_map/ppermute | solution.py:27
  146.0 2.0 add_multiply_fusion
  149.1 2.3 add_add_fusion.5
  153.4 75.6 %reduce-scatter.2.cloned.1.call-done = f32[2,8,512]{2,1,0:T(8,128)} async-done(((f32[2,128,512]{2,1,0:T(8,128)}), f32[2,8,512]{2,1,0:T(8,128)}) %reduce-scatter.2.cloned.1.call-update) | async-done | bytes 32784 | tf_op jit(solution)/shard_map/reduce_scatter | solution.py:148
  230.7 5.0 %all-to-all-start = ((f32[16,2,8,512]{3,2,1,0:T(8,128)}), f32[16,2,8,512]{3,2,1,0:T(8,128)S(1)}, u32[]{:S(2)}, u32[]{:S(2)}) async-start(f32[16,2,8,512]{3,2,1,0:T(8,128)} %stack.51), calls=%async_computation.1 | async-start | bytes 1048576 | tf_op jit(solution)/shard_map/all_to_all | solution.py:157
  235.7 25.2 %all_gather.6 = f32[2,128,512]{2,1,0:T(8,128)S(1)} all-gather(f32[2,8,512]{2,1,0:T(8,128)S(1)} %get-tuple-element.8), channel_id=1, replica_groups=mesh['scen'=16,'lx'=4,'ly'=4] {'scen'}, dimensions={1}, use_global_device_ids=true | all-gather | bytes 557056 | tf_op jit(solution)/shard_map/all_gather | solution.py:159
  260.9 22.9 %all_gather.7 = f32[2,128,512]{2,1,0:T(8,128)S(1)} all-gather(f32[2,8,512]{2,1,0:T(8,128)S(1)} %get-tuple-element.9), channel_id=1, replica_groups=mesh['scen'=16,'lx'=4,'ly'=4] {'scen'}, dimensions={1}, use_global_device_ids=true | all-gather | bytes 557056 | tf_op jit(solution)/shard_map/all_gather | solution.py:160
  (79 shorter events, 36.1 us)
Async XLA Ops:
  7.2 8.7 %copy-start.1 = (s32[128,512]{1,0:T(8,128)S(1)}, s32[128,512]{1,0:T(8,128)}, u32[]{:S(2)}) copy-start(s32[128,512]{1,0:T(8,128)} %param.17) | copy-start | bytes 786436
  7.2 8.7 %copy-start.2 = (f32[1,128,512]{2,1,0:T(8,128)S(1)}, f32[1,128,512]{2,1,0:T(8,128)}, u32[]{:S(2)}) copy-start(f32[1,128,512]{2,1,0:T(8,128)} %param.14) | copy-start | bytes 786436
  7.2 8.7 %copy-start = (f32[2,128,512]{2,1,0:T(8,128)S(1)}, f32[2,128,512]{2,1,0:T(8,128)}, u32[]{:S(2)}) copy-start(f32[2,128,512]{2,1,0:T(8,128)} %param.18) | copy-start | bytes 1572868
  7.2 221.8 %reduce-scatter.2.cloned.1.call-start = ((), (), s32[]{:S(2)}) async-start(), calls=%async_computation.2 | async-start | bytes 557056 | tf_op jit(solution)/shard_map/reduce_scatter | solution.py:148
  10.3 11.3 %collective-permute-start = (f32[3,2,512]{2,1,0:T(2,128)S(1)}, f32[3,2,512]{2,1,0:T(2,128)S(1)}, u32[]{:S(2)}, u32[]{:S(2)}) collective-permute-start(f32[3,2,512]{2,1,0:T(2,128)S(1)} %get-tuple-element.119), channel_id=1, source_target_pairs={{0,4},{4,8},{8,12},{1,5},{5,9},{9,13},{2,6},{6,10},{10,14},{3,7},{... | collective-permute-start | bytes 36872 | tf_op jit(solution)/shard_map/ppermute | solution.py:24
  12.2 16.0 %copy-start.4 = (s32[1,128]{1,0:T(1,128)S(1)}, s32[1,128]{1,0:T(1,128)}, u32[]{:S(2)}) copy-start(s32[1,128]{1,0:T(1,128)} %param.16) | copy-start | bytes 1540
  12.2 9.3 %collective-permute-start.1 = (f32[3,2,512]{2,1,0:T(2,128)S(1)}, f32[3,2,512]{2,1,0:T(2,128)S(1)}, u32[]{:S(2)}, u32[]{:S(2)}) collective-permute-start(f32[3,2,512]{2,1,0:T(2,128)S(1)} %get-tuple-element.120), channel_id=1, source_target_pairs={{4,0},{8,4},{12,8},{5,1},{9,5},{13,9},{6,2},{10,6},{14,10},{7,3},{... | collective-permute-start | bytes 36872 | tf_op jit(solution)/shard_map/ppermute | solution.py:27
  15.9 22.3 %collective-permute-start.4 = (f32[4,2,512]{2,1,0:T(2,128)S(1)}, f32[4,2,512]{2,1,0:T(2,128)S(1)}, u32[]{:S(2)}, u32[]{:S(2)}) collective-permute-start(f32[4,2,512]{2,1,0:T(2,128)S(1)} %get-tuple-element.85), channel_id=1, source_target_pairs={{0,4},{4,8},{8,12},{1,5},{5,9},{9,13},{2,6},{6,10},{10,14},{3,7},{... | collective-permute-start | bytes 49160 | tf_op jit(solution)/shard_map/ppermute | solution.py:24
  17.9 20.3 %collective-permute-start.5 = (f32[4,2,512]{2,1,0:T(2,128)S(1)}, f32[4,2,512]{2,1,0:T(2,128)S(1)}, u32[]{:S(2)}, u32[]{:S(2)}) collective-permute-start(f32[4,2,512]{2,1,0:T(2,128)S(1)} %get-tuple-element.86), channel_id=1, source_target_pairs={{4,0},{8,4},{12,8},{5,1},{9,5},{13,9},{6,2},{10,6},{14,10},{7,3},{... | collective-permute-start | bytes 49160 | tf_op jit(solution)/shard_map/ppermute | solution.py:27
  21.7 12.7 %collective-permute-start.2 = (f32[3,132,2]{2,1,0:T(8,128)S(1)}, f32[3,132,2]{2,1,0:T(8,128)S(1)}, u32[]{:S(2)}, u32[]{:S(2)}) collective-permute-start(f32[3,132,2]{2,1,0:T(8,128)S(1)} %get-tuple-element.109), channel_id=1, source_target_pairs={{0,1},{1,2},{2,3},{4,5},{5,6},{6,7},{8,9},{9,10},{10,11},{12,13},{... | collective-permute-start | bytes 9512 | tf_op jit(solution)/shard_map/ppermute | solution.py:24
  26.9 10.5 %collective-permute-start.3 = (f32[3,132,2]{2,1,0:T(8,128)S(1)}, f32[3,132,2]{2,1,0:T(8,128)S(1)}, u32[]{:S(2)}, u32[]{:S(2)}) collective-permute-start(f32[3,132,2]{2,1,0:T(8,128)S(1)} %get-tuple-element.110), channel_id=1, source_target_pairs={{1,0},{2,1},{3,2},{5,4},{6,5},{7,6},{9,8},{10,9},{11,10},{13,12},{... | collective-permute-start | bytes 9512 | tf_op jit(solution)/shard_map/ppermute | solution.py:27
  38.4 17.6 %collective-permute-start.6 = (f32[4,132,2]{2,1,0:T(8,128)S(1)}, f32[4,132,2]{2,1,0:T(8,128)S(1)}, u32[]{:S(2)}, u32[]{:S(2)}) collective-permute-start(f32[4,132,2]{2,1,0:T(8,128)S(1)} %get-tuple-element.83), channel_id=1, source_target_pairs={{0,1},{1,2},{2,3},{4,5},{5,6},{6,7},{8,9},{9,10},{10,11},{12,13},{... | collective-permute-start | bytes 12680 | tf_op jit(solution)/shard_map/ppermute | solution.py:24
  46.5 15.3 %collective-permute-start.7 = (f32[4,132,2]{2,1,0:T(8,128)S(1)}, f32[4,132,2]{2,1,0:T(8,128)S(1)}, u32[]{:S(2)}, u32[]{:S(2)}) collective-permute-start(f32[4,132,2]{2,1,0:T(8,128)S(1)} %get-tuple-element.84), channel_id=1, source_target_pairs={{1,0},{2,1},{3,2},{5,4},{6,5},{7,6},{9,8},{10,9},{11,10},{13,12},{... | collective-permute-start | bytes 12680 | tf_op jit(solution)/shard_map/ppermute | solution.py:27
  62.7 1.0 copy-start.3
  65.1 5.6 %collective-permute-start.8 = (f32[3,2,512]{2,1,0:T(2,128)S(1)}, f32[3,2,512]{2,1,0:T(2,128)S(1)}, u32[]{:S(2)}, u32[]{:S(2)}) collective-permute-start(f32[3,2,512]{2,1,0:T(2,128)S(1)} %get-tuple-element.117), channel_id=1, source_target_pairs={{0,4},{4,8},{8,12},{1,5},{5,9},{9,13},{2,6},{6,10},{10,14},{3,7},{... | collective-permute-start | bytes 36872 | tf_op jit(solution)/shard_map/ppermute | solution.py:24
  67.1 5.0 %collective-permute-start.9 = (f32[3,2,512]{2,1,0:T(2,128)S(1)}, f32[3,2,512]{2,1,0:T(2,128)S(1)}, u32[]{:S(2)}, u32[]{:S(2)}) collective-permute-start(f32[3,2,512]{2,1,0:T(2,128)S(1)} %get-tuple-element.118), channel_id=1, source_target_pairs={{4,0},{8,4},{12,8},{5,1},{9,5},{13,9},{6,2},{10,6},{14,10},{7,3},{... | collective-permute-start | bytes 36872 | tf_op jit(solution)/shard_map/ppermute | solution.py:27
  72.3 10.4 %collective-permute-start.10 = (f32[3,132,2]{2,1,0:T(8,128)S(1)}, f32[3,132,2]{2,1,0:T(8,128)S(1)}, u32[]{:S(2)}, u32[]{:S(2)}) collective-permute-start(f32[3,132,2]{2,1,0:T(8,128)S(1)} %get-tuple-element.107), channel_id=1, source_target_pairs={{0,1},{1,2},{2,3},{4,5},{5,6},{6,7},{8,9},{9,10},{10,11},{12,13},{... | collective-permute-start | bytes 9512 | tf_op jit(solution)/shard_map/ppermute | solution.py:24
  75.3 12.6 %collective-permute-start.11 = (f32[3,132,2]{2,1,0:T(8,128)S(1)}, f32[3,132,2]{2,1,0:T(8,128)S(1)}, u32[]{:S(2)}, u32[]{:S(2)}) collective-permute-start(f32[3,132,2]{2,1,0:T(8,128)S(1)} %get-tuple-element.108), channel_id=1, source_target_pairs={{1,0},{2,1},{3,2},{5,4},{6,5},{7,6},{9,8},{10,9},{11,10},{13,12},{... | collective-permute-start | bytes 9512 | tf_op jit(solution)/shard_map/ppermute | solution.py:27
  90.5 5.8 %collective-permute-start.12 = (f32[3,1,512]{2,1,0:T(1,128)S(1)}, f32[3,1,512]{2,1,0:T(1,128)S(1)}, u32[]{:S(2)}, u32[]{:S(2)}) collective-permute-start(f32[3,1,512]{2,1,0:T(1,128)S(1)} %get-tuple-element.147), channel_id=1, source_target_pairs={{0,4},{4,8},{8,12},{1,5},{5,9},{9,13},{2,6},{6,10},{10,14},{3,7},{... | collective-permute-start | bytes 18440 | tf_op jit(solution)/shard_map/ppermute | solution.py:24
  92.4 5.0 %collective-permute-start.13 = (f32[3,1,512]{2,1,0:T(1,128)S(1)}, f32[3,1,512]{2,1,0:T(1,128)S(1)}, u32[]{:S(2)}, u32[]{:S(2)}) collective-permute-start(f32[3,1,512]{2,1,0:T(1,128)S(1)} %get-tuple-element.148), channel_id=1, source_target_pairs={{4,0},{8,4},{12,8},{5,1},{9,5},{13,9},{6,2},{10,6},{14,10},{7,3},{... | collective-permute-start | bytes 18440 | tf_op jit(solution)/shard_map/ppermute | solution.py:27
  97.5 10.5 %collective-permute-start.14 = (f32[3,130,1]{2,1,0:T(8,128)S(1)}, f32[3,130,1]{2,1,0:T(8,128)S(1)}, u32[]{:S(2)}, u32[]{:S(2)}) collective-permute-start(f32[3,130,1]{2,1,0:T(8,128)S(1)} %get-tuple-element.113), channel_id=1, source_target_pairs={{0,1},{1,2},{2,3},{4,5},{5,6},{6,7},{8,9},{9,10},{10,11},{12,13},{... | collective-permute-start | bytes 4688 | tf_op jit(solution)/shard_map/ppermute | solution.py:24
  100.7 12.7 %collective-permute-start.15 = (f32[3,130,1]{2,1,0:T(8,128)S(1)}, f32[3,130,1]{2,1,0:T(8,128)S(1)}, u32[]{:S(2)}, u32[]{:S(2)}) collective-permute-start(f32[3,130,1]{2,1,0:T(8,128)S(1)} %get-tuple-element.114), channel_id=1, source_target_pairs={{1,0},{2,1},{3,2},{5,4},{6,5},{7,6},{9,8},{10,9},{11,10},{13,12},{... | collective-permute-start | bytes 4688 | tf_op jit(solution)/shard_map/ppermute | solution.py:27
  122.7 5.7 %collective-permute-start.16 = (f32[3,1,512]{2,1,0:T(1,128)S(1)}, f32[3,1,512]{2,1,0:T(1,128)S(1)}, u32[]{:S(2)}, u32[]{:S(2)}) collective-permute-start(f32[3,1,512]{2,1,0:T(1,128)S(1)} %get-tuple-element.115), channel_id=1, source_target_pairs={{0,4},{4,8},{8,12},{1,5},{5,9},{9,13},{2,6},{6,10},{10,14},{3,7},{... | collective-permute-start | bytes 18440 | tf_op jit(solution)/shard_map/ppermute | solution.py:24
  124.7 5.0 %collective-permute-start.17 = (f32[3,1,512]{2,1,0:T(1,128)S(1)}, f32[3,1,512]{2,1,0:T(1,128)S(1)}, u32[]{:S(2)}, u32[]{:S(2)}) collective-permute-start(f32[3,1,512]{2,1,0:T(1,128)S(1)} %get-tuple-element.116), channel_id=1, source_target_pairs={{4,0},{8,4},{12,8},{5,1},{9,5},{13,9},{6,2},{10,6},{14,10},{7,3},{... | collective-permute-start | bytes 18440 | tf_op jit(solution)/shard_map/ppermute | solution.py:27
  129.8 10.5 %collective-permute-start.18 = (f32[3,130,1]{2,1,0:T(8,128)S(1)}, f32[3,130,1]{2,1,0:T(8,128)S(1)}, u32[]{:S(2)}, u32[]{:S(2)}) collective-permute-start(f32[3,130,1]{2,1,0:T(8,128)S(1)} %get-tuple-element.111), channel_id=1, source_target_pairs={{0,1},{1,2},{2,3},{4,5},{5,6},{6,7},{8,9},{9,10},{10,11},{12,13},{... | collective-permute-start | bytes 4688 | tf_op jit(solution)/shard_map/ppermute | solution.py:24
  132.9 12.7 %collective-permute-start.19 = (f32[3,130,1]{2,1,0:T(8,128)S(1)}, f32[3,130,1]{2,1,0:T(8,128)S(1)}, u32[]{:S(2)}, u32[]{:S(2)}) collective-permute-start(f32[3,130,1]{2,1,0:T(8,128)S(1)} %get-tuple-element.112), channel_id=1, source_target_pairs={{1,0},{2,1},{3,2},{5,4},{6,5},{7,6},{9,8},{10,9},{11,10},{13,12},{... | collective-permute-start | bytes 4688 | tf_op jit(solution)/shard_map/ppermute | solution.py:27
  230.7 53.0 %all-to-all-start = ((f32[16,2,8,512]{3,2,1,0:T(8,128)}), f32[16,2,8,512]{3,2,1,0:T(8,128)S(1)}, u32[]{:S(2)}, u32[]{:S(2)}) async-start(f32[16,2,8,512]{3,2,1,0:T(8,128)} %stack.51), calls=%async_computation.1 | async-start | bytes 1048576 | tf_op jit(solution)/shard_map/all_to_all | solution.py:157
Sparse Core Ops, SparseCore 0:
  153.5 75.4 reduce-scatter.1
